TPU v7x, 128 devices: a whole 4x4x4 slice. The times are simulated.
128 devices in a mesh: section: 8 (over z_lo, y), dp: 16 (over z_hi, x, core).
Axes of the slice: x: 4, y: 4, z: 4 (z_hi: 2, z_lo: 2; z = z_hi * 2 + z_lo), core: 2. Of those that a mesh axis runs over, the one named last changes fastest.
Arguments:
- enc_in: bfloat16 [8, 2, 8192, 1152], P('section', None, 'dp'), may hold values from -6 to 6
- dec_in: bfloat16 [8, 2, 8192, 1152], P('section', None, 'dp'), may hold values from -6 to 6
- cotangent: bfloat16 [8, 2, 8192, 1152], P('section', None, 'dp'), may hold values from -0.23925781 to 0.23925781
- w_proj: float32 [8, 1152, 1152], P('section', 'dp'), may hold values from -0.1875 to 0.1875
- w_skip: float32 [8, 2304, 1152], P('section', 'dp'), may hold values from -0.125 to 0.125
- m_proj: float32 [8, 1152, 1152], P('section', 'dp'), may hold values from -3 to 3
- v_proj: float32 [8, 1152, 1152], P('section', 'dp'), may hold values from 0.05 to 1
- m_skip: float32 [8, 2304, 1152], P('section', 'dp'), may hold values from -3 to 3
- v_skip: float32 [8, 2304, 1152], P('section', 'dp'), may hold values from 0.05 to 1
Outputs:
- dec_out: bfloat16 [8, 2, 8192, 1152], P('section', None, 'dp')
- enc_grad: bfloat16 [8, 2, 8192, 1152], P('section', None, 'dp')
- dec_grad: bfloat16 [8, 2, 8192, 1152], P('section', None, 'dp')
- new_w_proj: float32 [8, 1152, 1152], P('section', 'dp')
- new_m_proj: float32 [8, 1152, 1152], P('section', 'dp')
- new_v_proj: float32 [8, 1152, 1152], P('section', 'dp')
- new_w_skip: float32 [8, 2304, 1152], P('section', 'dp')
- new_m_skip: float32 [8, 2304, 1152], P('section', 'dp')
- new_v_skip: float32 [8, 2304, 1152], P('section', 'dp')
All inputs are finite; a program needn't handle non-finite values.
Results may differ from a plain program's by a relative error of at most 0.025.
Values may be sent and summed in bfloat16 or wider, within the bound.
A program may use at most 128 MiB of HBM per device.

v0:
```python
import jax
import jax.numpy as jnp
from jax import lax
from jax.sharding import PartitionSpec as P

half_root = 0.7071067811865476
gauss_norm = 0.3989422804014327
beta_one = 0.9
beta_two = 0.95
learn_rate = 0.002
adam_eps = 1e-08
correct_one = 1.0 - 0.9**10
correct_two = 1.0 - 0.95**10


def swapped(value, axis, bit):
    mask = 2**bit
    pairs = [(source, source ^ mask) for source in range(lax.axis_size(axis))]
    return lax.ppermute(value, axis, pairs)


def in_blocks(value, dim, count):
    before, after = (value.shape[:dim], value.shape[dim + 1 :])
    return jnp.moveaxis(value.reshape(*before, count, -1, *after), dim, 0)


def one_scatter(arrays, axis, dims):
    count = lax.axis_size(axis)
    pieces = [in_blocks(a, dim, count) for a, dim in zip(arrays, dims)]
    lines = jnp.concatenate([b.reshape(count, -1) for b in pieces], axis=1)
    span = max(16, -(-lines.shape[1] // 1024) * 8)
    lines = jnp.pad(lines, ((0, 0), (0, span * 128 - lines.shape[1]))).reshape(-1, 128)
    ravelled, at, outs = (lax.psum_scatter(lines, axis, tiled=True).reshape(-1), 0, [])
    for b in pieces:
        part = b[0]
        outs.append(ravelled[at : at + part.size].reshape(part.shape))
        at += part.size
    return tuple(outs)


def gelu_parts(preact):
    normal_cdf = 0.5 * (1.0 + lax.erf(preact * half_root))
    density = jnp.exp(-0.5 * preact * preact) * gauss_norm
    return (preact * normal_cdf, normal_cdf + preact * density)


def adam_update(weight, moment, second, grad):
    new_moment = beta_one * moment + (1.0 - beta_one) * grad
    new_second = beta_two * second + (1.0 - beta_two) * grad * grad
    step_size = new_moment / correct_one / (jnp.sqrt(new_second / correct_two) + adam_eps)
    return (weight - learn_rate * step_size, new_moment, new_second)


def top_bit():
    return lax.axis_size("section").bit_length() - 2


def send_forward(value):
    return swapped(value, "section", top_bit())


def send_backward(value):
    return swapped(value, "section", top_bit())


def layer_pass(enc_rows, dec_rows, out_grad, proj_full, skip_full):
    width = enc_rows.shape[1]
    skip_local = jnp.dot(enc_rows, proj_full, preferred_element_type=jnp.float32).astype(
        jnp.bfloat16
    )
    skip_remote = send_forward(skip_local)
    joined = jnp.concatenate([dec_rows, skip_remote], axis=1)
    preact = jnp.dot(joined, skip_full, preferred_element_type=jnp.float32)
    activated, gelu_slope = gelu_parts(preact)
    dec_out = activated.astype(jnp.bfloat16)
    pre_grad = (out_grad.astype(jnp.float32) * gelu_slope).astype(jnp.bfloat16)
    input_grad = jnp.einsum("rk,jk->rj", pre_grad, skip_full, preferred_element_type=jnp.float32)
    dec_grad = input_grad[:, :width].astype(jnp.bfloat16)
    skip_sent = input_grad[:, width:].astype(jnp.bfloat16)
    skip_grad = send_backward(skip_sent)
    enc_grad = jnp.einsum(
        "rk,jk->rj", skip_grad, proj_full, preferred_element_type=jnp.float32
    ).astype(jnp.bfloat16)
    grad_proj = jnp.einsum("rj,rk->jk", enc_rows, skip_grad, preferred_element_type=jnp.float32)
    grad_skip = jnp.einsum("rj,rk->jk", joined, pre_grad, preferred_element_type=jnp.float32)
    return (dec_out, enc_grad, dec_grad, grad_proj, grad_skip)


def body(enc_in, dec_in, cotangent, w_proj, w_skip, m_proj, v_proj, m_skip, v_skip):
    proj_all, skip_all = (
        lax.all_gather(w_proj.astype(jnp.bfloat16), "dp", axis=1, tiled=True),
        lax.all_gather(w_skip.astype(jnp.bfloat16), "dp", axis=1, tiled=True),
    )
    proj_full = proj_all[0]
    skip_full = skip_all[0]
    micro = enc_in.shape[1]
    tokens_here = enc_in.shape[2]
    width = enc_in.shape[3]
    rows = micro * tokens_here
    result = layer_pass(
        enc_in[0].reshape(rows, width),
        dec_in[0].reshape(rows, width),
        cotangent[0].reshape(rows, width),
        proj_full,
        skip_full,
    )
    dec_out = result[0].reshape(micro, tokens_here, width)
    enc_grad = result[1].reshape(micro, tokens_here, width)
    dec_grad = result[2].reshape(micro, tokens_here, width)
    proj_sum, skip_sum = tuple(
        (
            part.astype(jnp.float32)
            for part in one_scatter(
                (result[3].astype(jnp.bfloat16), result[4].astype(jnp.bfloat16)), "dp", (0, 0)
            )
        )
    )
    new_w_proj, new_m_proj, new_v_proj = adam_update(w_proj[0], m_proj[0], v_proj[0], proj_sum)
    new_w_skip, new_m_skip, new_v_skip = adam_update(w_skip[0], m_skip[0], v_skip[0], skip_sum)
    return (
        dec_out[None],
        enc_grad[None],
        dec_grad[None],
        new_w_proj[None],
        new_m_proj[None],
        new_v_proj[None],
        new_w_skip[None],
        new_m_skip[None],
        new_v_skip[None],
    )


def solution(mesh):
    in_specs = (
        P("section", None, "dp", None),
        P("section", None, "dp", None),
        P("section", None, "dp", None),
        P("section", "dp", None),
        P("section", "dp", None),
        P("section", "dp", None),
        P("section", "dp", None),
        P("section", "dp", None),
        P("section", "dp", None),
    )
    out_specs = (
        P("section", None, "dp", None),
        P("section", None, "dp", None),
        P("section", None, "dp", None),
        P("section", "dp", None),
        P("section", "dp", None),
        P("section", "dp", None),
        P("section", "dp", None),
        P("section", "dp", None),
        P("section", "dp", None),
    )
    return jax.shard_map(body, mesh=mesh, in_specs=in_specs, out_specs=out_specs, check_vma=False)
```

profile of v0, /device:TPU:0, one launch (start us, length us, event | category | flops | bytes accessed | tf_op | source)
XLA Modules:
  0.0 429.5 jit_solution(92079628465543061)
XLA Ops:
  7.2 0.0 copy-start
  7.2 0.0 all-gather.3.cloned.1.call-start
  7.2 1.8 convert_element_type.71
  9.0 0.0 all-gather.3.cloned.1.call-update
  9.1 0.0 all-gather.5.cloned.1.call-start
  9.1 1.9 convert_element_type.73
  11.0 0.0 all-gather.5.cloned.1.call-update
  11.0 0.0 all-reduce.3.cloned.1.call-start
  11.1 52.7 %all-gather.3.cloned.1.call-done = bf16[1,1152,1152]{2,1,0:T(8,128)(2,1)} async-done(((bf16[1,72,1152]{2,1,0:T(8,128)(2,1)}), bf16[1,1152,1152]{2,1,0:T(8,128)(2,1)}) %all-gather.3.cloned.1.call-update) | async-done | bytes 2654224 | tf_op jit(solution)/shard_map/all_gather | solution.py:91
  63.7 0.0 copy-done
  63.7 5.4 %convolution_convert_fusion.4 = bf16[1024,1152]{1,0:T(8,128)(2,1)S(1)} fusion(bf16[1024,1152]{1,0:T(8,128)(2,1)S(1)} %bitcast.29, bf16[1,1152,1152]{2,1,0:T(8,128)(2,1)} %all-gather.3.cloned.1.call-done), kind=kOutput, calls=%fused_computation.19 | convolution fusion | flops 2719088640 | bytes 7372800 | tf_op jit(solution)/shard_map/dot_general | solution.py:68
  69.2 0.7 collective-permute-start
  69.9 70.6 %collective-permute-done = bf16[1024,1152]{1,0:T(8,128)(2,1)} collective-permute-done((bf16[1024,1152]{1,0:T(8,128)(2,1)S(1)}, bf16[1024,1152]{1,0:T(8,128)(2,1)}, u32[]{:S(2)}, u32[]{:S(2)}) %collective-permute-start) | collective-permute-done | bytes 2359328 | tf_op jit(solution)/shard_map/ppermute | solution.py:19
  140.5 1.6 all-gather.5.cloned.1.call-done
  142.1 0.0 copy-start.3
  142.1 13.2 %fusion.9 = (bf16[1024,1152]{1,0:T(8,128)(2,1)S(1)}, bf16[1024,1152]{1,0:T(8,128)(2,1)}) fusion(bf16[1,2,512,1152]{3,2,1,0:T(8,128)(2,1)} %param.11, bf16[1,2304,1152]{2,1,0:T(8,128)(2,1)} %all-gather.5.cloned.1.call-done, bf16[1024,1152]{1,0:T(8,128)(2,1)} %collective-permute-done, bf16[1024,1152]{1,0:T(8,128)(2,1)} %bitcast.32), kind=kOutput, calls=%fused_computation.14 | convolution fusion | flops 5460590592 | bytes 17104896 | tf_op jit(solution)/shard_map/dot_general | solution.py:73
  155.3 0.0 copy-done.3
  155.3 6.5 %convolution_convert_fusion.2 = bf16[1024,2304]{1,0:T(8,128)(2,1)S(1)} fusion(bf16[1024,1152]{1,0:T(8,128)(2,1)S(1)} %get-tuple-element.17, bf16[1,2304,1152]{2,1,0:T(8,128)(2,1)S(1)} %copy-done.3), kind=kOutput, calls=%fused_computation.5 | convolution fusion | flops 5438177280 | bytes 12386304 | tf_op jit(solution)/shard_map/rk,jk->rj/dot_general | solution.py:77
  161.9 0.0 copy-start.4
  161.9 2.5 fusion.18
  164.4 0.7 collective-permute-start.1
  165.1 0.0 copy-done.4
  165.1 8.4 %convolution_convert_fusion = bf16[2304,1152]{1,0:T(8,128)(2,1)} fusion(bf16[1024,1152]{1,0:T(8,128)(2,1)S(1)} %get-tuple-element.17, bf16[1024,1152]{1,0:T(8,128)(2,1)} %collective-permute-done, bf16[1024,1152]{1,0:T(8,128)(2,1)S(1)} %bitcast.33), kind=kOutput, calls=%fused_computation | convolution fusion | flops 5447909376 | bytes 12386304 | tf_op jit(solution)/shard_map/rj,rk->jk/dot_general | solution.py:85
  173.5 5.7 %reshape_reshape.7 = bf16[16,165888]{1,0:T(8,128)(2,1)} reshape(bf16[2304,1152]{1,0:T(8,128)(2,1)} %convolution_convert_fusion) | data formatting | bytes 10616832 | tf_op jit(solution)/shard_map/reshape;reshape | solution.py:30
  179.2 39.0 %collective-permute-done.1 = bf16[1024,1152]{1,0:T(8,128)(2,1)} collective-permute-done((bf16[1024,1152]{1,0:T(8,128)(2,1)}, bf16[1024,1152]{1,0:T(8,128)(2,1)}, u32[]{:S(2)}, u32[]{:S(2)}) %collective-permute-start.1) | collective-permute-done | bytes 2359328 | tf_op jit(solution)/shard_map/ppermute | solution.py:19
  218.1 6.4 %fusion = bf16[1152,1152]{0,1:T(8,128)(2,1)} fusion(bf16[1024,1152]{1,0:T(8,128)(2,1)} %collective-permute-done.1, bf16[1024,1152]{1,0:T(8,128)(2,1)S(1)} %bitcast.30), kind=kOutput, calls=%fused_computation.4 | convolution fusion | flops 2719236096 | bytes 7372800 | tf_op jit(solution)/shard_map/rj,rk->jk/dot_general | solution.py:84
  224.5 5.2 %copy.19 = bf16[1152,1152]{1,0:T(8,128)(2,1)} copy(bf16[1152,1152]{0,1:T(8,128)(2,1)} %fusion) | data formatting | bytes 5308416 | tf_op jit(solution)/shard_map/convert_element_type | solution.py:114
  229.8 3.6 reshape_reshape.6
  233.4 8.3 %pad_maximum_fusion = bf16[16,248832]{1,0:T(8,128)(2,1)} fusion(bf16[16,165888]{1,0:T(8,128)(2,1)} %reshape_reshape.7, bf16[16,82944]{1,0:T(8,128)(2,1)} %reshape_reshape.6), kind=kLoop, calls=%fused_computation.1 | loop fusion | flops 15925248 | bytes 15925248 | tf_op jit(solution)/shard_map/concatenate | solution.py:30
  241.7 7.6 %reshape.82 = bf16[31104,128]{1,0:T(8,128)(2,1)} reshape(bf16[16,248832]{1,0:T(8,128)(2,1)} %pad_maximum_fusion) | data formatting | bytes 15925248 | tf_op jit(solution)/shard_map/reshape | solution.py:32
  249.3 0.0 copy-start.5
  249.3 0.0 all-reduce.3.cloned.1.call-update
  249.3 0.6 copy-done.5
  250.0 0.6 dynamic-slice
  251.2 0.0 copy-start.2
  251.2 7.4 %convolution_convert_fusion.3 = bf16[1024,1152]{1,0:T(8,128)(2,1)} fusion(bf16[1024,1152]{1,0:T(8,128)(2,1)} %collective-permute-done.1, bf16[1,1152,1152]{2,1,0:T(8,128)(2,1)} %all-gather.3.cloned.1.call-done), kind=kOutput, calls=%fused_computation.18 | convolution fusion | flops 2719088640 | bytes 7372800 | tf_op jit(solution)/shard_map/rk,jk->rj/dot_general | solution.py:81
  258.7 0.0 copy-start.1
  258.7 151.7 %all-reduce.3.cloned.1.call-done = bf16[31104,128]{1,0:T(8,128)(2,1)} async-done(((bf16[31104,128]{1,0:T(8,128)(2,1)}), bf16[31104,128]{1,0:T(8,128)(2,1)}) %all-reduce.3.cloned.1.call-update) | async-done | bytes 7962640
  410.3 1.7 dynamic-slice_convert_fusion.1
  412.0 1.8 reshape.84
  413.8 1.9 dynamic-slice_convert_fusion
  415.6 2.1 reshape.85
  417.7 0.0 copy-done.2
  417.7 2.3 multiply_subtract_fusion.1
  419.9 0.0 copy-done.1
  419.9 3.0 multiply_subtract_fusion
Async XLA Ops:
  7.2 56.6 %copy-start = (bf16[1,2,512,1152]{3,2,1,0:T(8,128)(2,1)S(1)}, bf16[1,2,512,1152]{3,2,1,0:T(8,128)(2,1)}, u32[]{:S(2)}) copy-start(bf16[1,2,512,1152]{3,2,1,0:T(8,128)(2,1)} %param.9) | copy-start | bytes 7077892
  7.2 56.6 %all-gather.3.cloned.1.call-start = ((), (), s32[]{:S(2)}) async-start(), calls=%async_computation | async-start | bytes 2820096 | tf_op jit(solution)/shard_map/all_gather | solution.py:91
  9.1 133.1 %all-gather.5.cloned.1.call-start = ((), (), s32[]{:S(2)}) async-start(), calls=%async_computation.1 | async-start | bytes 5640192 | tf_op jit(solution)/shard_map/all_gather | solution.py:92
  11.0 399.3 %all-reduce.3.cloned.1.call-start = ((), (), s32[]{:S(2)}) async-start(), calls=%async_computation.2 | async-start | bytes 15925248
  69.2 71.3 %collective-permute-start = (bf16[1024,1152]{1,0:T(8,128)(2,1)S(1)}, bf16[1024,1152]{1,0:T(8,128)(2,1)}, u32[]{:S(2)}, u32[]{:S(2)}) collective-permute-start(bf16[1024,1152]{1,0:T(8,128)(2,1)S(1)} %convolution_convert_fusion.4), channel_id=1, source_target_pairs={{0,64},{16,80},{32,96},{48,112},{64,0},{80,16},{96,32},{112,48},{1... | collective-permute-start | bytes 7077896 | tf_op jit(solution)/shard_map/ppermute | solution.py:19
  142.1 13.2 %copy-start.3 = (bf16[1,2304,1152]{2,1,0:T(8,128)(2,1)S(1)}, bf16[1,2304,1152]{2,1,0:T(8,128)(2,1)}, u32[]{:S(2)}) copy-start(bf16[1,2304,1152]{2,1,0:T(8,128)(2,1)} %all-gather.5.cloned.1.call-done) | copy-start | bytes 15925252
  161.9 3.2 copy-start.4
  164.4 53.7 %collective-permute-start.1 = (bf16[1024,1152]{1,0:T(8,128)(2,1)}, bf16[1024,1152]{1,0:T(8,128)(2,1)}, u32[]{:S(2)}, u32[]{:S(2)}) collective-permute-start(bf16[1024,1152]{1,0:T(8,128)(2,1)} %get-tuple-element.16), channel_id=1, source_target_pairs={{0,64},{16,80},{32,96},{48,112},{64,0},{80,16},{96,32},{112,48},{1... | collective-permute-start | bytes 7077896 | tf_op jit(solution)/shard_map/ppermute | solution.py:19
  249.3 0.7 copy-start.5
  251.2 166.5 %copy-start.2 = (f32[1,72,1152]{2,1,0:T(8,128)S(1)}, f32[1,72,1152]{2,1,0:T(8,128)}, u32[]{:S(2)}) copy-start(f32[1,72,1152]{2,1,0:T(8,128)} %param.12) | copy-start | bytes 995332
  258.7 161.3 %copy-start.1 = (f32[1,144,1152]{2,1,0:T(8,128)S(1)}, f32[1,144,1152]{2,1,0:T(8,128)}, u32[]{:S(2)}) copy-start(f32[1,144,1152]{2,1,0:T(8,128)} %param.13) | copy-start | bytes 1990660
Sparse Core Ops, SparseCore 0:
  11.0 52.6 all-gather.2
  66.7 75.4 all-gather.4
  249.5 160.8 all-reduce.2
where the time goes:
time: 430 us
  waiting for transfers between devices  316 us (73%)
  matrix products  47.4 us (11%)
  local copies, waits for them, and re-layouts  29.8 us (7%)
  other arithmetic  20.8 us (5%)
  between operations  14.5 us (3%)
    unnamed x4, waiting for transfers between devices  152 us
    ppermute x2, waiting for transfers between devices, swapped(): return lax.ppermute(value, axis, pairs)  110 us
    all_gather x1, waiting for transfers between devices, body(): lax.all_gather(w_proj.astype(jnp.bfloat16), 'dp', axis=1, tiled=True)  52.7 us
    dot_general x1, matrix products, layer_pass(): preact = jnp.dot(joined, skip_full, preferred_element_type=jnp.float32)  13.2 us
    another operation x2, local copies, waits for them, and re-layouts, one_scatter(): lines = jnp.concatenate([b.reshape(count, -1) for b in pieces], axis=1)  9.3 us
  transfers between devices with their start and end apart: 5, of which 5 were waited for; matrix products, arithmetic and copies ran while one was open for 7% of the time, Pallas kernels for 0%

commit v1 on v0

--- a/solution.py
+++ b/solution.py
@@ -88,7 +88,12 @@
 
 def body(enc_in, dec_in, cotangent, w_proj, w_skip, m_proj, v_proj, m_skip, v_skip):
     proj_all, skip_all = (
-        lax.all_gather(w_proj.astype(jnp.bfloat16), "dp", axis=1, tiled=True),
+        jnp.concatenate(
+            lax.all_to_all(
+                jnp.stack([w_proj.astype(jnp.bfloat16)] * lax.axis_size("dp")), "dp", 0, 0
+            ),
+            axis=1,
+        ),
         lax.all_gather(w_skip.astype(jnp.bfloat16), "dp", axis=1, tiled=True),
     )
     proj_full = proj_all[0]

time: 430 us -> 416 us (0.967)
  waiting for transfers between devices: 316 us -> 256 us
  blocking collectives: 0 us -> 48.3 us
    all_gather x1 -> x0, waiting for transfers between devices: 52.7 us -> none  [body(): lax.all_gather(w_proj.astype(jnp.bfloat16), 'dp', axis=1, tiled=True)]
    all_to_all x0 -> x1, blocking collectives: none -> 48.3 us  [body(): lax.all_to_all(jnp.stack([w_proj.astype(jnp.bfloat16)] * lax.axis_size('d...]
    ppermute x2, waiting for transfers between devices: 110 us -> 104 us  [swapped(): return lax.ppermute(value, axis, pairs)]
    unnamed x4 -> x3, waiting for transfers between devices: 152 us -> 152 us
  transfers between devices with their start and end apart: 5 -> 4, of which waited for: 5 -> 3; matrix products, arithmetic and copies ran while one was open for 7% -> 7% of each run, Pallas kernels for 0% -> 0%
where the time goes in v1:
time: 416 us; the launch traced here: 415 us
  waiting for transfers between devices  256 us (62%)
  blocking collectives  48.3 us (12%)
  matrix products  45 us (11%)
  local copies, waits for them, and re-layouts  30 us (7%)
  other arithmetic  20.1 us (5%)
  between operations  14.8 us (4%)
    unnamed x3, waiting for transfers between devices  152 us
    ppermute x2, waiting for transfers between devices, swapped(): return lax.ppermute(value, axis, pairs)  104 us
    all_to_all x1, blocking collectives, body(): lax.all_to_all(jnp.stack([w_proj.astype(jnp.bfloat16)] * lax.axis_size('d...  48.3 us
    dot_general x1, matrix products, layer_pass(): preact = jnp.dot(joined, skip_full, preferred_element_type=jnp.float32)  12.6 us
    another operation x2, local copies, waits for them, and re-layouts, one_scatter(): lines = jnp.concatenate([b.reshape(count, -1) for b in pieces], axis=1)  9.31 us
    dot_general x1, matrix products, layer_pass(): jnp.einsum('rj,rk->jk', joined, pre_grad, preferred_element_type=jnp.floa...  8.36 us
  transfers between devices with their start and end apart: 4, of which 3 were waited for; matrix products, arithmetic and copies ran while one was open for 7% of the time, Pallas kernels for 0%

profile of v1, /device:TPU:0, one launch (start us, length us, event | category | flops | bytes accessed | tf_op | source)
XLA Modules:
  0.0 415.1 jit_solution(13920154905683651702)
XLA Ops:
  7.2 0.0 copy-start
  7.2 0.0 all-gather.2.cloned.1.call-start
  7.2 2.0 convert_element_type.76
  9.2 0.0 all-gather.2.cloned.1.call-update
  9.3 0.0 all-reduce.3.cloned.1.call-start
  9.3 1.0 convert_bitcast_fusion
  10.3 0.2 stack.2
  10.5 48.3 %all_to_all.5 = bf16[16,1,72,1152]{3,2,1,0:T(8,128)(2,1)S(1)} all-to-all(bf16[16,1,72,1152]{3,2,1,0:T(8,128)(2,1)S(1)} %stack.2), channel_id=1, replica_groups=mesh['section'=8,'dp'=16] {'dp'}, dimensions={0} | all-to-all | bytes 5308416 | tf_op jit(solution)/shard_map/all_to_all | solution.py:92
  58.8 0.0 copy-done
  58.8 0.0 copy-start.2
  58.8 3.7 convolution_convert_fusion.4
  62.5 0.0 copy-done.2
  62.5 1.1 collective-permute-start
  63.6 64.8 %collective-permute-done = bf16[1024,1152]{1,0:T(8,128)(2,1)} collective-permute-done((bf16[1024,1152]{1,0:T(8,128)(2,1)S(1)}, bf16[1024,1152]{1,0:T(8,128)(2,1)}, u32[]{:S(2)}, u32[]{:S(2)}) %collective-permute-start) | collective-permute-done | bytes 2359328 | tf_op jit(solution)/shard_map/ppermute | solution.py:19
  128.4 0.0 all-gather.2.cloned.1.call-done
  128.4 0.0 copy-start.4
  128.4 12.6 %fusion.9 = (bf16[1024,1152]{1,0:T(8,128)(2,1)S(1)}, bf16[1024,1152]{1,0:T(8,128)(2,1)}) fusion(bf16[1,2,512,1152]{3,2,1,0:T(8,128)(2,1)} %param.11, bf16[1,2304,1152]{2,1,0:T(8,128)(2,1)} %all-gather.2.cloned.1.call-done, bf16[1024,1152]{1,0:T(8,128)(2,1)} %collective-permute-done, bf16[1024,1152]{1,0:T(8,128)(2,1)} %bitcast.34), kind=kOutput, calls=%fused_computation.14 | convolution fusion | flops 5460590592 | bytes 17104896 | tf_op jit(solution)/shard_map/dot_general | solution.py:73
  141.0 0.0 copy-done.4
  141.0 6.5 %convolution_convert_fusion.2 = bf16[1024,2304]{1,0:T(8,128)(2,1)S(1)} fusion(bf16[1024,1152]{1,0:T(8,128)(2,1)S(1)} %get-tuple-element.17, bf16[1,2304,1152]{2,1,0:T(8,128)(2,1)S(1)} %copy-done.4), kind=kOutput, calls=%fused_computation.5 | convolution fusion | flops 5438177280 | bytes 12386304 | tf_op jit(solution)/shard_map/rk,jk->rj/dot_general | solution.py:77
  147.5 0.0 copy-start.5
  147.5 2.5 fusion.16
  150.0 0.3 collective-permute-start.1
  150.3 0.0 copy-done.5
  150.3 8.4 %convolution_convert_fusion = bf16[2304,1152]{1,0:T(8,128)(2,1)} fusion(bf16[1024,1152]{1,0:T(8,128)(2,1)S(1)} %get-tuple-element.17, bf16[1024,1152]{1,0:T(8,128)(2,1)} %collective-permute-done, bf16[1024,1152]{1,0:T(8,128)(2,1)S(1)} %bitcast.35), kind=kOutput, calls=%fused_computation | convolution fusion | flops 5447909376 | bytes 12386304 | tf_op jit(solution)/shard_map/rj,rk->jk/dot_general | solution.py:85
  158.7 5.7 %reshape_reshape.7 = bf16[16,165888]{1,0:T(8,128)(2,1)} reshape(bf16[2304,1152]{1,0:T(8,128)(2,1)} %convolution_convert_fusion) | data formatting | bytes 10616832 | tf_op jit(solution)/shard_map/reshape;reshape | solution.py:30
  164.4 39.0 %collective-permute-done.1 = bf16[1024,1152]{1,0:T(8,128)(2,1)} collective-permute-done((bf16[1024,1152]{1,0:T(8,128)(2,1)}, bf16[1024,1152]{1,0:T(8,128)(2,1)}, u32[]{:S(2)}, u32[]{:S(2)}) %collective-permute-start.1) | collective-permute-done | bytes 2359328 | tf_op jit(solution)/shard_map/ppermute | solution.py:19
  203.4 6.4 %fusion = bf16[1152,1152]{0,1:T(8,128)(2,1)} fusion(bf16[1024,1152]{1,0:T(8,128)(2,1)} %collective-permute-done.1, bf16[1024,1152]{1,0:T(8,128)(2,1)S(1)} %bitcast.30), kind=kOutput, calls=%fused_computation.4 | convolution fusion | flops 2719236096 | bytes 7372800 | tf_op jit(solution)/shard_map/rj,rk->jk/dot_general | solution.py:84
  209.8 5.2 %copy.19 = bf16[1152,1152]{1,0:T(8,128)(2,1)} copy(bf16[1152,1152]{0,1:T(8,128)(2,1)} %fusion) | data formatting | bytes 5308416 | tf_op jit(solution)/shard_map/convert_element_type | solution.py:119
  215.0 3.6 reshape_reshape.6
  218.6 8.3 %pad_maximum_fusion = bf16[16,248832]{1,0:T(8,128)(2,1)} fusion(bf16[16,165888]{1,0:T(8,128)(2,1)} %reshape_reshape.7, bf16[16,82944]{1,0:T(8,128)(2,1)} %reshape_reshape.6), kind=kLoop, calls=%fused_computation.1 | loop fusion | flops 15925248 | bytes 15925248 | tf_op jit(solution)/shard_map/concatenate | solution.py:30
  226.9 7.6 %reshape.85 = bf16[31104,128]{1,0:T(8,128)(2,1)} reshape(bf16[16,248832]{1,0:T(8,128)(2,1)} %pad_maximum_fusion) | data formatting | bytes 15925248 | tf_op jit(solution)/shard_map/reshape | solution.py:32
  234.6 0.0 copy-start.6
  234.6 0.0 all-reduce.3.cloned.1.call-update
  234.6 0.6 copy-done.6
  235.2 0.6 dynamic-slice
  236.5 0.0 copy-start.3
  236.5 7.4 %convolution_convert_fusion.3 = bf16[1024,1152]{1,0:T(8,128)(2,1)} fusion(bf16[1024,1152]{1,0:T(8,128)(2,1)} %collective-permute-done.1, bf16[1152,1152]{1,0:T(8,128)(2,1)} %bitcast.32), kind=kOutput, calls=%fused_computation.18 | convolution fusion | flops 2719088640 | bytes 7372800 | tf_op jit(solution)/shard_map/rk,jk->rj/dot_general | solution.py:81
  243.9 0.0 copy-start.1
  243.9 151.7 %all-reduce.3.cloned.1.call-done = bf16[31104,128]{1,0:T(8,128)(2,1)} async-done(((bf16[31104,128]{1,0:T(8,128)(2,1)}), bf16[31104,128]{1,0:T(8,128)(2,1)}) %all-reduce.3.cloned.1.call-update) | async-done | bytes 7962640
  395.6 1.7 dynamic-slice_convert_fusion.1
  397.3 1.8 reshape.87
  399.1 1.9 dynamic-slice_convert_fusion
  401.0 2.1 reshape.88
  403.0 0.0 copy-done.3
  403.0 2.3 multiply_subtract_fusion.1
  405.3 0.0 copy-done.1
  405.3 3.0 multiply_subtract_fusion
Async XLA Ops:
  7.2 51.6 %copy-start = (bf16[1,2,512,1152]{3,2,1,0:T(8,128)(2,1)S(1)}, bf16[1,2,512,1152]{3,2,1,0:T(8,128)(2,1)}, u32[]{:S(2)}) copy-start(bf16[1,2,512,1152]{3,2,1,0:T(8,128)(2,1)} %param.9) | copy-start | bytes 7077892
  7.2 121.2 %all-gather.2.cloned.1.call-start = ((), (), s32[]{:S(2)}) async-start(), calls=%async_computation.1 | async-start | bytes 5640192 | tf_op jit(solution)/shard_map/all_gather | solution.py:97
  9.3 386.4 %all-reduce.3.cloned.1.call-start = ((), (), s32[]{:S(2)}) async-start(), calls=%async_computation.2 | async-start | bytes 15925248
  58.8 3.8 copy-start.2
  62.5 65.9 %collective-permute-start = (bf16[1024,1152]{1,0:T(8,128)(2,1)S(1)}, bf16[1024,1152]{1,0:T(8,128)(2,1)}, u32[]{:S(2)}, u32[]{:S(2)}) collective-permute-start(bf16[1024,1152]{1,0:T(8,128)(2,1)S(1)} %convolution_convert_fusion.4), channel_id=1, source_target_pairs={{0,64},{16,80},{32,96},{48,112},{64,0},{80,16},{96,32},{112,48},{1... | collective-permute-start | bytes 7077896 | tf_op jit(solution)/shard_map/ppermute | solution.py:19
  128.4 12.6 %copy-start.4 = (bf16[1,2304,1152]{2,1,0:T(8,128)(2,1)S(1)}, bf16[1,2304,1152]{2,1,0:T(8,128)(2,1)}, u32[]{:S(2)}) copy-start(bf16[1,2304,1152]{2,1,0:T(8,128)(2,1)} %all-gather.2.cloned.1.call-done) | copy-start | bytes 15925252
  147.5 2.8 copy-start.5
  150.0 53.3 %collective-permute-start.1 = (bf16[1024,1152]{1,0:T(8,128)(2,1)}, bf16[1024,1152]{1,0:T(8,128)(2,1)}, u32[]{:S(2)}, u32[]{:S(2)}) collective-permute-start(bf16[1024,1152]{1,0:T(8,128)(2,1)} %get-tuple-element.16), channel_id=1, source_target_pairs={{0,64},{16,80},{32,96},{48,112},{64,0},{80,16},{96,32},{112,48},{1... | collective-permute-start | bytes 7077896 | tf_op jit(solution)/shard_map/ppermute | solution.py:19
  234.6 0.7 copy-start.6
  236.5 166.6 %copy-start.3 = (f32[1,72,1152]{2,1,0:T(8,128)S(1)}, f32[1,72,1152]{2,1,0:T(8,128)}, u32[]{:S(2)}) copy-start(f32[1,72,1152]{2,1,0:T(8,128)} %param.12) | copy-start | bytes 995332
  243.9 161.4 %copy-start.1 = (f32[1,144,1152]{2,1,0:T(8,128)S(1)}, f32[1,144,1152]{2,1,0:T(8,128)}, u32[]{:S(2)}) copy-start(f32[1,144,1152]{2,1,0:T(8,128)} %param.13) | copy-start | bytes 1990660
Sparse Core Ops, SparseCore 0:
  10.9 92.7 all-gather.1
  234.7 160.8 all-reduce.2
